TPU v7x, 512 devices: a whole 4x8x8 slice. The times are simulated.
512 devices in a mesh: chan: 8 (over z), sx: 8 (over x, core), sy: 8 (over y).
Axes of the slice: x: 4, y: 8, z: 8, core: 2. Of those that a mesh axis runs over, the one named last changes fastest.
Arguments:
- volume: bfloat16 [8, 64, 64, 256], P('sx', 'sy', None, 'chan'), may hold values from -6 to 6
- kernel: bfloat16 [27, 256, 256], P(None, 'chan'), may hold values from -0.078125 to 0.078125
- grad_out: bfloat16 [8, 64, 64, 256], P('sx', 'sy', None, 'chan'), may hold values from -6 to 6
Outputs:
- out: bfloat16 [8, 64, 64, 256], P('sx', 'sy', None, 'chan')
- grad_input: bfloat16 [8, 64, 64, 256], P('sx', 'sy', None, 'chan')
- grad_kernel: float32 [27, 256, 256], P(None, 'chan')
All inputs are finite; a program needn't handle non-finite values.
Results may differ from a plain program's by a relative error of at most 0.0015.
Values may be sent and summed in bfloat16 or wider, within the bound.
No kernel may reach another device: no remote copies, remote signals or barrier semaphores. Data moves between devices by JAX's collectives and lax.ppermute only.
A program may use at most 64 MiB of HBM per device.

v0:
```python
import math
import jax
import jax.numpy as jnp
from jax import lax
from jax.sharding import PartitionSpec as P


def padded_2(shard, sides, width):
    for axis, dim in sides:
        count, length = (lax.axis_size(axis), shard.shape[dim])
        up = [(i, (i + 1) % count) for i in range(count - 1)]
        down = [(j, i) for i, j in up]
        last = lax.slice_in_dim(shard, length - width, length, axis=dim)
        leading = lax.slice_in_dim(shard, 0, width, axis=dim)
        before = lax.ppermute(last, axis, up)
        after = lax.ppermute(leading, axis, down)
        shard = jnp.concatenate([before, shard, after], axis=dim)
    return shard


def body(volume, kernel, grad_out):
    size_x, size_y, size_z, own_in = volume.shape
    total_out = kernel.shape[2]
    cells = size_x * size_y * size_z
    rim = padded_2(volume, (("sx", 0), ("sy", 1)), 1)
    padded = jnp.pad(rim, ((0, 0), (0, 0), (1, 1), (0, 0)))
    offsets = [(index // 9, index // 3 % 3, index % 3) for index in range(27)]
    partial_out = jnp.zeros((cells, total_out), jnp.float32)
    for index in range(27):
        a, b, e = offsets[index]
        window = padded[a : a + size_x, b : b + size_y, e : e + size_z].reshape(cells, own_in)
        partial_out = partial_out + jnp.dot(
            window, kernel[index], preferred_element_type=jnp.float32
        )
    partial_out = partial_out.reshape(size_x, size_y, size_z, total_out)
    out = lax.psum_scatter(partial_out, "chan", scatter_dimension=3, tiled=True).astype(
        jnp.bfloat16
    )
    grad_full = lax.all_gather(grad_out, "chan", axis=3, tiled=True)
    grad_rimmed = padded_2(grad_full, (("sx", 0), ("sy", 1)), 1)
    grad_padded = jnp.pad(grad_rimmed, ((0, 0), (0, 0), (1, 1), (0, 0)))
    flat_grad = grad_full.reshape(cells, total_out)
    back = jnp.zeros((cells, own_in), jnp.float32)
    kernel_terms = []
    for index in range(27):
        a, b, e = offsets[index]
        window = grad_padded[
            2 - a : 2 - a + size_x, 2 - b : 2 - b + size_y, 2 - e : 2 - e + size_z
        ].reshape(cells, total_out)
        back = back + lax.dot_general(
            window, kernel[index], (((1,), (1,)), ((), ())), preferred_element_type=jnp.float32
        )
        in_window = padded[a : a + size_x, b : b + size_y, e : e + size_z].reshape(cells, own_in)
        kernel_terms.append(
            lax.dot_general(
                in_window, flat_grad, (((0,), (0,)), ((), ())), preferred_element_type=jnp.float32
            )
        )
    grad_input = back.reshape(size_x, size_y, size_z, own_in).astype(jnp.bfloat16)
    local_kernel = jnp.stack(kernel_terms)
    summed = lax.psum(local_kernel, ("sx", "sy"))
    all_cells = cells * lax.axis_size("sx") * lax.axis_size("sy")
    grad_kernel = summed / jnp.float32(math.sqrt(all_cells))
    return (out, grad_input, grad_kernel)


def solution(mesh):
    return jax.shard_map(
        body,
        mesh=mesh,
        in_specs=(P("sx", "sy", None, "chan"), P(None, "chan", None), P("sx", "sy", None, "chan")),
        out_specs=(P("sx", "sy", None, "chan"), P("sx", "sy", None, "chan"), P(None, "chan", None)),
        check_vma=False,
    )
```

profile of v0, /device:TPU:25, one launch (start us, length us, event | category | flops | bytes accessed | tf_op | source)
XLA Modules:
  0.0 342.9 jit_solution(3898932481704692713)
XLA Ops:
  8.1 3.7 %collective-permute-start = (bf16[1,8,64,32]{2,3,1,0:T(8,128)(2,1)}, bf16[1,8,64,32]{2,3,1,0:T(8,128)(2,1)S(1)}, u32[]{:S(2)}, u32[]{:S(2)}) collective-permute-start(bf16[1,8,64,32]{2,3,1,0:T(8,128)(2,1)} %param.3), channel_id=1, source_target_pairs={{0,8},{8,16},{16,24},{24,32},{32,40},{40,48},{48,56},{1,9},{9,17},... | collective-permute-start | bytes 98312 | tf_op jit(solution)/shard_map/ppermute | solution.py:15
  11.7 1.9 collective-permute-start.1
  15.5 2.1 collective-permute-done.1
  17.6 2.1 collective-permute-start.3
  19.7 4.4 %collective-permute-start.2 = (bf16[3,1,64,32]{2,3,1,0:T(8,128)(2,1)S(1)}, bf16[3,1,64,32]{2,3,1,0:T(8,128)(2,1)S(1)}, u32[]{:S(2)}, u32[]{:S(2)}) collective-permute-start(bf16[3,1,64,32]{2,3,1,0:T(8,128)(2,1)S(1)} %get-tuple-element.68), channel_id=1, source_target_pairs={{0,1},{1,2},{2,3},{3,4},{4,5},{5,6},{6,7},{8,9},{9,10},{10,11},{11... | collective-permute-start | bytes 36872 | tf_op jit(solution)/shard_map/ppermute | solution.py:15
  24.1 26.2 %all_gather.3 = bf16[1,8,64,256]{2,1,0,3:T(8,128)(2,1)S(1)} all-gather(bf16[1,8,64,32]{2,1,0,3:T(8,128)(2,1)S(1)} %copy.98), channel_id=1, replica_groups=mesh['chan'=8,'sx'=8,'sy'=8] {'chan'}, dimensions={3}, use_global_device_ids=true | all-gather | bytes 294912 | tf_op jit(solution)/shard_map/all_gather | solution.py:39
  50.6 5.5 %collective-permute-start.5 = (bf16[1,8,64,256]{3,2,1,0:T(8,128)(2,1)S(1)}, bf16[1,8,64,256]{3,2,1,0:T(8,128)(2,1)S(1)}, u32[]{:S(2)}, u32[]{:S(2)}) collective-permute-start(bf16[1,8,64,256]{3,2,1,0:T(8,128)(2,1)S(1)} %copy.99), channel_id=1, source_target_pairs={{8,0},{16,8},{24,16},{32,24},{40,32},{48,40},{56,48},{9,1},{17,9},... | collective-permute-start | bytes 786440 | tf_op jit(solution)/shard_map/ppermute | solution.py:16
  56.1 4.7 %collective-permute-start.4 = (bf16[1,8,64,256]{3,2,1,0:T(8,128)(2,1)S(1)}, bf16[1,8,64,256]{3,2,1,0:T(8,128)(2,1)S(1)}, u32[]{:S(2)}, u32[]{:S(2)}) collective-permute-start(bf16[1,8,64,256]{3,2,1,0:T(8,128)(2,1)S(1)} %copy.99), channel_id=1, source_target_pairs={{0,8},{8,16},{16,24},{24,32},{32,40},{40,48},{48,56},{1,9},{9,17},... | collective-permute-start | bytes 786440 | tf_op jit(solution)/shard_map/ppermute | solution.py:15
  63.9 1.1 fusion.241
  67.0 1.4 pad_maximum_fusion.13
  73.0 1.5 copy.76
  74.5 1.6 reshape.329
  76.1 1.5 copy.77
  77.6 1.6 reshape.330
  79.2 1.5 copy.78
  80.6 1.6 reshape.331
  82.2 1.5 copy.79
  83.7 1.6 reshape.332
  85.9 1.6 reshape.333
  88.1 1.6 reshape.334
  90.3 1.6 reshape.335
  91.9 1.5 copy.84
  93.4 1.6 reshape.337
  95.0 1.5 copy.85
  96.4 1.6 reshape.338
  98.7 1.6 reshape.339
  100.9 1.6 reshape.340
  102.4 1.5 copy.88
  103.9 1.6 reshape.341
  106.1 1.6 reshape.342
  107.7 1.5 copy.90
  109.2 1.6 reshape.343
  110.7 1.5 copy.91
  112.2 1.6 reshape.344
  114.5 1.6 reshape.347
  116.8 0.9 fusion.35
  119.3 0.9 fusion.32
  121.9 0.9 fusion.29
  124.4 0.9 fusion.26
  126.9 0.9 fusion.23
  129.4 0.9 fusion.20
  146.8 1.9 collective-permute-start.7
  148.7 4.8 %collective-permute-start.6 = (bf16[3,1,64,256]{3,2,1,0:T(8,128)(2,1)S(1)}, bf16[3,1,64,256]{3,2,1,0:T(8,128)(2,1)S(1)}, u32[]{:S(2)}, u32[]{:S(2)}) collective-permute-start(bf16[3,1,64,256]{3,2,1,0:T(8,128)(2,1)S(1)} %get-tuple-element.39), channel_id=1, source_target_pairs={{0,1},{1,2},{2,3},{3,4},{4,5},{5,6},{6,7},{8,9},{9,10},{10,11},{11... | collective-permute-start | bytes 294920 | tf_op jit(solution)/shard_map/ppermute | solution.py:15
  153.8 1.3 copy.97
  155.8 0.9 fusion.240
  162.8 168.9 %all-reduce.4.cloned.1.call-done = f32[27,32,256]{2,1,0:T(8,128)} async-done(((f32[27,32,256]{2,1,0:T(8,128)}), f32[27,32,256]{2,1,0:T(8,128)}) %all-reduce.4.cloned.1.call-update) | async-done | bytes 884752 | tf_op jit(solution)/shard_map/psum | solution.py:61
  331.7 2.2 broadcast_multiply_fusion
  333.9 1.5 convert_element_type.21
  (205 shorter events, 48.3 us)
Async XLA Ops:
  8.0 52.8 %copy-start.4 = (bf16[1,8,64,32]{2,3,1,0:T(8,128)(2,1)S(1)}, bf16[1,8,64,32]{2,3,1,0:T(8,128)(2,1)}, u32[]{:S(2)}) copy-start(bf16[1,8,64,32]{2,3,1,0:T(8,128)(2,1)} %param.3) | copy-start | bytes 98308
  8.0 323.7 %all-reduce.4.cloned.1.call-start = ((), (), s32[]{:S(2)}) async-start(), calls=%async_computation.2 | async-start | bytes 1769472 | tf_op jit(solution)/shard_map/psum | solution.py:61
  8.1 6.5 %collective-permute-start = (bf16[1,8,64,32]{2,3,1,0:T(8,128)(2,1)}, bf16[1,8,64,32]{2,3,1,0:T(8,128)(2,1)S(1)}, u32[]{:S(2)}, u32[]{:S(2)}) collective-permute-start(bf16[1,8,64,32]{2,3,1,0:T(8,128)(2,1)} %param.3), channel_id=1, source_target_pairs={{0,8},{8,16},{16,24},{24,32},{32,40},{40,48},{48,56},{1,9},{9,17},... | collective-permute-start | bytes 98312 | tf_op jit(solution)/shard_map/ppermute | solution.py:15
  11.7 5.8 %collective-permute-start.1 = (bf16[1,8,64,32]{2,3,1,0:T(8,128)(2,1)}, bf16[1,8,64,32]{2,3,1,0:T(8,128)(2,1)S(1)}, u32[]{:S(2)}, u32[]{:S(2)}) collective-permute-start(bf16[1,8,64,32]{2,3,1,0:T(8,128)(2,1)} %param.3), channel_id=1, source_target_pairs={{8,0},{16,8},{24,16},{32,24},{40,32},{48,40},{56,48},{9,1},{17,9},... | collective-permute-start | bytes 98312 | tf_op jit(solution)/shard_map/ppermute | solution.py:16
  14.6 47.1 %copy-start.8 = (bf16[1,8,64,32]{2,3,1,0:T(8,128)(2,1)}, bf16[1,8,64,32]{2,3,1,0:T(8,128)(2,1)S(1)}, u32[]{:S(2)}) copy-start(bf16[1,8,64,32]{2,3,1,0:T(8,128)(2,1)S(1)} %collective-permute-done) | copy-start | bytes 98308
  17.5 45.0 %copy-start.6 = (bf16[1,8,64,32]{2,3,1,0:T(8,128)(2,1)}, bf16[1,8,64,32]{2,3,1,0:T(8,128)(2,1)S(1)}, u32[]{:S(2)}) copy-start(bf16[1,8,64,32]{2,3,1,0:T(8,128)(2,1)S(1)} %collective-permute-done.1) | copy-start | bytes 98308
  17.6 44.9 %collective-permute-start.3 = (bf16[3,1,64,32]{2,3,1,0:T(8,128)(2,1)S(1)}, bf16[3,1,64,32]{2,3,1,0:T(8,128)(2,1)S(1)}, u32[]{:S(2)}, u32[]{:S(2)}) collective-permute-start(bf16[3,1,64,32]{2,3,1,0:T(8,128)(2,1)S(1)} %get-tuple-element.69), channel_id=1, source_target_pairs={{1,0},{2,1},{3,2},{4,3},{5,4},{6,5},{7,6},{9,8},{10,9},{11,10},{12... | collective-permute-start | bytes 36872 | tf_op jit(solution)/shard_map/ppermute | solution.py:16
  19.7 42.9 %collective-permute-start.2 = (bf16[3,1,64,32]{2,3,1,0:T(8,128)(2,1)S(1)}, bf16[3,1,64,32]{2,3,1,0:T(8,128)(2,1)S(1)}, u32[]{:S(2)}, u32[]{:S(2)}) collective-permute-start(bf16[3,1,64,32]{2,3,1,0:T(8,128)(2,1)S(1)} %get-tuple-element.68), channel_id=1, source_target_pairs={{0,1},{1,2},{2,3},{3,4},{4,5},{5,6},{6,7},{8,9},{9,10},{10,11},{11... | collective-permute-start | bytes 36872 | tf_op jit(solution)/shard_map/ppermute | solution.py:15
  50.6 96.1 %collective-permute-start.5 = (bf16[1,8,64,256]{3,2,1,0:T(8,128)(2,1)S(1)}, bf16[1,8,64,256]{3,2,1,0:T(8,128)(2,1)S(1)}, u32[]{:S(2)}, u32[]{:S(2)}) collective-permute-start(bf16[1,8,64,256]{3,2,1,0:T(8,128)(2,1)S(1)} %copy.99), channel_id=1, source_target_pairs={{8,0},{16,8},{24,16},{32,24},{40,32},{48,40},{56,48},{9,1},{17,9},... | collective-permute-start | bytes 786440 | tf_op jit(solution)/shard_map/ppermute | solution.py:16
  56.1 90.7 %collective-permute-start.4 = (bf16[1,8,64,256]{3,2,1,0:T(8,128)(2,1)S(1)}, bf16[1,8,64,256]{3,2,1,0:T(8,128)(2,1)S(1)}, u32[]{:S(2)}, u32[]{:S(2)}) collective-permute-start(bf16[1,8,64,256]{3,2,1,0:T(8,128)(2,1)S(1)} %copy.99), channel_id=1, source_target_pairs={{0,8},{8,16},{16,24},{24,32},{32,40},{40,48},{48,56},{1,9},{9,17},... | collective-permute-start | bytes 786440 | tf_op jit(solution)/shard_map/ppermute | solution.py:15
  62.5 0.6 copy-start.36
  63.1 0.6 copy-start.37
  63.9 2.3 copy-start
  68.5 0.6 copy-start.2
  68.5 18.9 %copy-start.14 = (bf16[1,8,64,32]{2,3,1,0:T(8,128)(2,1)S(1)}, bf16[1,8,64,32]{2,3,1,0:T(8,128)(2,1)}, u32[]{:S(2)}) copy-start(bf16[1,8,64,32]{2,3,1,0:T(8,128)(2,1)} %get-tuple-element.51) | copy-start | bytes 98308
  68.5 21.2 %copy-start.13 = (bf16[1,8,64,32]{2,3,1,0:T(8,128)(2,1)S(1)}, bf16[1,8,64,32]{2,3,1,0:T(8,128)(2,1)}, u32[]{:S(2)}) copy-start(bf16[1,8,64,32]{2,3,1,0:T(8,128)(2,1)} %get-tuple-element.50) | copy-start | bytes 98308
  74.5 25.7 %copy-start.12 = (bf16[1,8,64,32]{2,3,1,0:T(8,128)(2,1)S(1)}, bf16[1,8,64,32]{2,3,1,0:T(8,128)(2,1)}, u32[]{:S(2)}) copy-start(bf16[1,8,64,32]{2,3,1,0:T(8,128)(2,1)} %get-tuple-element.47) | copy-start | bytes 98308
  88.1 25.7 %copy-start.11 = (bf16[1,8,64,32]{2,3,1,0:T(8,128)(2,1)S(1)}, bf16[1,8,64,32]{2,3,1,0:T(8,128)(2,1)}, u32[]{:S(2)}) copy-start(bf16[1,8,64,32]{2,3,1,0:T(8,128)(2,1)} %get-tuple-element.42) | copy-start | bytes 98308
  90.3 25.7 %copy-start.3 = (bf16[1,8,64,32]{2,3,1,0:T(8,128)(2,1)S(1)}, bf16[1,8,64,32]{2,3,1,0:T(8,128)(2,1)}, u32[]{:S(2)}) copy-start(bf16[1,8,64,32]{2,3,1,0:T(8,128)(2,1)} %copy-done.2) | copy-start | bytes 98308
  102.4 16.1 %copy-start.9 = (bf16[1,8,64,32]{2,3,1,0:T(8,128)(2,1)S(1)}, bf16[1,8,64,32]{2,3,1,0:T(8,128)(2,1)}, u32[]{:S(2)}) copy-start(bf16[1,8,64,32]{2,3,1,0:T(8,128)(2,1)} %copy-done.8) | copy-start | bytes 98308
  116.0 5.0 %copy-start.1 = (bf16[1,8,64,32]{2,3,1,0:T(8,128)(2,1)S(1)}, bf16[1,8,64,32]{2,3,1,0:T(8,128)(2,1)}, u32[]{:S(2)}) copy-start(bf16[1,8,64,32]{2,3,1,0:T(8,128)(2,1)} %get-tuple-element.60) | copy-start | bytes 98308
  121.0 5.0 %copy-start.5 = (bf16[1,8,64,32]{2,3,1,0:T(8,128)(2,1)S(1)}, bf16[1,8,64,32]{2,3,1,0:T(8,128)(2,1)}, u32[]{:S(2)}) copy-start(bf16[1,8,64,32]{2,3,1,0:T(8,128)(2,1)} %param.3) | copy-start | bytes 98308
  128.6 5.0 %copy-start.7 = (bf16[1,8,64,32]{2,3,1,0:T(8,128)(2,1)S(1)}, bf16[1,8,64,32]{2,3,1,0:T(8,128)(2,1)}, u32[]{:S(2)}) copy-start(bf16[1,8,64,32]{2,3,1,0:T(8,128)(2,1)} %copy-done.6) | copy-start | bytes 98308
  134.4 3.5 %copy-start.17 = (bf16[512,32]{0,1:T(8,128)(2,1)S(1)}, bf16[512,32]{0,1:T(8,128)(2,1)}, u32[]{:S(2)}) copy-start(bf16[512,32]{0,1:T(8,128)(2,1)} %reshape.324) | copy-start | bytes 98308
  136.9 1.2 copy-start.21
  137.8 0.8 copy-start.25
  137.8 196.1 %reduce-scatter.2.cloned.1.call-start = ((), (), s32[]{:S(2)}) async-start(), calls=%async_computation.1 | async-start | bytes 1179648 | tf_op jit(solution)/shard_map/reduce_scatter | solution.py:36
  138.2 0.8 copy-start.16
  138.6 0.8 copy-start.18
  138.9 0.8 copy-start.19
  139.3 0.8 copy-start.20
  139.7 0.8 copy-start.22
  140.1 0.8 copy-start.23
  140.4 0.8 copy-start.26
  140.9 0.8 copy-start.29
  141.2 0.8 copy-start.15
  141.6 0.8 copy-start.24
  142.0 0.8 copy-start.27
  142.4 0.8 copy-start.28
  142.7 0.8 copy-start.30
  143.2 0.8 copy-start.32
  143.5 0.8 copy-start.33
  143.9 0.8 copy-start.34
  144.3 0.8 copy-start.35
  145.0 0.8 copy-start.31
  145.8 0.8 copy-start.10
  146.8 8.3 %collective-permute-start.7 = (bf16[3,1,64,256]{3,2,1,0:T(8,128)(2,1)S(1)}, bf16[3,1,64,256]{3,2,1,0:T(8,128)(2,1)S(1)}, u32[]{:S(2)}, u32[]{:S(2)}) collective-permute-start(bf16[3,1,64,256]{3,2,1,0:T(8,128)(2,1)S(1)} %get-tuple-element.40), channel_id=1, source_target_pairs={{1,0},{2,1},{3,2},{4,3},{5,4},{6,5},{7,6},{9,8},{10,9},{11,10},{12... | collective-permute-start | bytes 294920 | tf_op jit(solution)/shard_map/ppermute | solution.py:16
  148.7 6.4 %collective-permute-start.6 = (bf16[3,1,64,256]{3,2,1,0:T(8,128)(2,1)S(1)}, bf16[3,1,64,256]{3,2,1,0:T(8,128)(2,1)S(1)}, u32[]{:S(2)}, u32[]{:S(2)}) collective-permute-start(bf16[3,1,64,256]{3,2,1,0:T(8,128)(2,1)S(1)} %get-tuple-element.39), channel_id=1, source_target_pairs={{0,1},{1,2},{2,3},{3,4},{4,5},{5,6},{6,7},{8,9},{9,10},{10,11},{11... | collective-permute-start | bytes 294920 | tf_op jit(solution)/shard_map/ppermute | solution.py:15
Sparse Core Ops, SparseCore 0:
  137.9 193.7 all-reduce.3
Sparse Core Ops, SparseCore 1:
  155.2 32.7 reduce-scatter.1
where the time goes:
time: 345 us; the launch traced here: 343 us
  waiting for transfers between devices  171 us (50%)
  local copies, waits for them, and re-layouts  60 us (17%)
  matrix products  34.2 us (10%)
  starting transfers between devices  29 us (8%)
  blocking collectives  26.2 us (8%)
  between operations  16.2 us (5%)
  other arithmetic  6.23 us (2%)
    psum x1, waiting for transfers between devices, body(): summed = lax.psum(local_kernel, ('sx', 'sy'))  169 us
    reshape x27, local copies, waits for them, and re-layouts, body(): padded[a:a + size_x, b:b + size_y, e:e + size_z].reshape(cells, own_in)  29.3 us
    all_gather x1, blocking collectives, body(): grad_full = lax.all_gather(grad_out, 'chan', axis=3, tiled=True)  26.2 us
    dot_general x27, matrix products, body(): lax.dot_general(in_window, flat_grad, (((0,), (0,)), ((), ())), preferred...  22.6 us
    slice x25, local copies, waits for them, and re-layouts, body(): padded[a:a + size_x, b:b + size_y, e:e + size_z].reshape(cells, own_in)  21 us
    ppermute x4, starting transfers between devices, padded_2(): before = lax.ppermute(last, axis, up)  17.6 us
    ppermute x4, starting transfers between devices, padded_2(): after = lax.ppermute(leading, axis, down)  11.4 us
    unnamed x81, local copies, waits for them, and re-layouts  6.98 us
  transfers between devices with their start and end apart: 10, of which 2 were waited for; matrix products, arithmetic and copies ran while one was open for 28% of the time, Pallas kernels for 0%

commit v1 on v0

--- a/solution.py
+++ b/solution.py
@@ -36,7 +36,11 @@
     out = lax.psum_scatter(partial_out, "chan", scatter_dimension=3, tiled=True).astype(
         jnp.bfloat16
     )
-    grad_full = lax.all_gather(grad_out, "chan", axis=3, tiled=True)
+    length_2 = lax.axis_size("chan")
+    repeats = [length_2 if d == 3 else 1 for d in range(grad_out.ndim)]
+    grad_full = lax.all_to_all(
+        jnp.tile(grad_out, repeats), "chan", split_axis=3, concat_axis=3, tiled=True
+    )
     grad_rimmed = padded_2(grad_full, (("sx", 0), ("sy", 1)), 1)
     grad_padded = jnp.pad(grad_rimmed, ((0, 0), (0, 0), (1, 1), (0, 0)))
     flat_grad = grad_full.reshape(cells, total_out)

time: 345 us -> 310 us (0.90)
  blocking collectives: 26.2 us -> 0 us
  matrix products: 34.2 us -> 17.5 us
  waiting for transfers between devices: 171 us -> 184 us
  local copies, waits for them, and re-layouts: 60 us -> 50.2 us
  starting transfers between devices: 29 us -> 34.4 us
    all_gather x1 -> x0, blocking collectives: 26.2 us -> none  [body(): grad_full = lax.all_gather(grad_out, 'chan', axis=3, tiled=True)]
    dot_general x27, matrix products: 22.6 us -> 5.83 us  [body(): lax.dot_general(in_window, flat_grad, (((0,), (0,)), ((), ())), preferred...]
    psum x1, waiting for transfers between devices: 169 us -> 180 us  [body(): summed = lax.psum(local_kernel, ('sx', 'sy'))]
    all_to_all x0 -> x1, starting transfers between devices: none -> 10 us  [body(): lax.all_to_all(jnp.tile(grad_out, repeats), 'chan', split_axis=3, concat_...]
    slice x25, local copies, waits for them, and re-layouts: 21 us -> 14.7 us  [body(): padded[a:a + size_x, b:b + size_y, e:e + size_z].reshape(cells, own_in)]
    reshape x27, local copies, waits for them, and re-layouts: 29.3 us -> 23.8 us  [body(): padded[a:a + size_x, b:b + size_y, e:e + size_z].reshape(cells, own_in)]
    ppermute x4, starting transfers between devices: 11.4 us -> 7.84 us  [padded_2(): after = lax.ppermute(leading, axis, down)]
    unnamed x81 -> x64, local copies, waits for them, and re-layouts: 6.98 us -> 7.61 us
  transfers between devices with their start and end apart: 10 -> 11, of which waited for: 2 -> 3; matrix products, arithmetic and copies ran while one was open for 28% -> 22% of each run, Pallas kernels for 0% -> 0%
where the time goes in v1:
time: 310 us; the launch traced here: 308 us
  waiting for transfers between devices  184 us (59%)
  local copies, waits for them, and re-layouts  50.2 us (16%)
  starting transfers between devices  34.4 us (11%)
  matrix products  17.5 us (6%)
  between operations  16.4 us (5%)
  other arithmetic  5.61 us (2%)
    psum x1, waiting for transfers between devices, body(): summed = lax.psum(local_kernel, ('sx', 'sy'))  180 us
    reshape x27, local copies, waits for them, and re-layouts, body(): padded[a:a + size_x, b:b + size_y, e:e + size_z].reshape(cells, own_in)  23.8 us
    ppermute x4, starting transfers between devices, padded_2(): before = lax.ppermute(last, axis, up)  16.5 us
    slice x25, local copies, waits for them, and re-layouts, body(): padded[a:a + size_x, b:b + size_y, e:e + size_z].reshape(cells, own_in)  14.7 us
    all_to_all x1, starting transfers between devices, body(): lax.all_to_all(jnp.tile(grad_out, repeats), 'chan', split_axis=3, concat_...  10 us
    ppermute x4, starting transfers between devices, padded_2(): after = lax.ppermute(leading, axis, down)  7.84 us
    unnamed x64, local copies, waits for them, and re-layouts  7.61 us
    dot_general x27, matrix products, body(): jnp.dot(window, kernel[index], preferred_element_type=jnp.float32)  6.65 us
  transfers between devices with their start and end apart: 11, of which 3 were waited for; matrix products, arithmetic and copies ran while one was open for 22% of the time, Pallas kernels for 0%

profile of v1, /device:TPU:25, one launch (start us, length us, event | category | flops | bytes accessed | tf_op | source)
XLA Modules:
  0.0 308.0 jit_solution(8132357685677638261)
XLA Ops:
  8.0 3.7 %collective-permute-start = (bf16[1,8,64,32]{2,3,1,0:T(8,128)(2,1)}, bf16[1,8,64,32]{2,3,1,0:T(8,128)(2,1)S(1)}, u32[]{:S(2)}, u32[]{:S(2)}) collective-permute-start(bf16[1,8,64,32]{2,3,1,0:T(8,128)(2,1)} %param.3), channel_id=1, source_target_pairs={{0,8},{8,16},{16,24},{24,32},{32,40},{40,48},{48,56},{1,9},{9,17},... | collective-permute-start | bytes 98312 | tf_op jit(solution)/shard_map/ppermute | solution.py:15
  11.7 1.9 collective-permute-start.1
  13.6 0.9 constant_dynamic-update-slice_fusion.1
  14.5 3.0 collective-permute-done.1
  17.5 2.1 collective-permute-start.3
  19.6 4.4 %collective-permute-start.2 = (bf16[3,1,64,32]{2,3,1,0:T(8,128)(2,1)S(1)}, bf16[3,1,64,32]{2,3,1,0:T(8,128)(2,1)S(1)}, u32[]{:S(2)}, u32[]{:S(2)}) collective-permute-start(bf16[3,1,64,32]{2,3,1,0:T(8,128)(2,1)S(1)} %get-tuple-element.68), channel_id=1, source_target_pairs={{0,1},{1,2},{2,3},{3,4},{4,5},{5,6},{6,7},{8,9},{9,10},{10,11},{11... | collective-permute-start | bytes 36872 | tf_op jit(solution)/shard_map/ppermute | solution.py:15
  24.0 0.9 tile.12
  25.3 1.1 reshape.439
  26.4 10.0 %all-to-all-start = ((bf16[8,2,8192]{2,1,0:T(2,128)(2,1)}), bf16[8,2,8192]{2,1,0:T(2,128)(2,1)S(1)}, u32[]{:S(2)}, u32[]{:S(2)}) async-start(bf16[8,2,8192]{2,1,0:T(2,128)(2,1)} %reshape.439), calls=%async_computation.1 | async-start | bytes 524288 | tf_op jit(solution)/shard_map/all_to_all | solution.py:41
  36.5 0.7 reshape.342
  37.3 0.7 reshape.333
  38.1 0.7 reshape.351
  40.2 1.0 fusion.241
  42.4 0.8 pad_maximum_fusion.13
  43.4 0.9 copy.72
  44.3 0.7 reshape.331
  45.0 0.9 copy.73
  45.9 0.7 reshape.332
  46.6 0.9 copy.76
  48.9 1.6 reshape.336
  50.5 1.5 copy.78
  52.0 1.6 reshape.337
  54.2 1.6 reshape.338
  56.4 1.6 reshape.339
  58.0 1.5 copy.81
  59.5 1.6 reshape.340
  61.1 1.5 copy.82
  62.6 1.6 reshape.341
  64.1 1.5 copy.84
  65.6 1.6 reshape.343
  67.2 1.5 copy.85
  68.7 1.6 reshape.344
  70.9 1.6 reshape.345
  73.1 1.6 reshape.346
  74.7 0.7 reshape.347
  75.6 0.7 reshape.349
  76.4 0.7 reshape.350
  77.3 0.7 reshape.354
  86.9 1.9 collective-permute-start.5
  88.8 3.6 %collective-permute-start.4 = (bf16[1,8,64,256]{3,2,1,0:T(8,128)(2,1)S(1)}, bf16[1,8,64,256]{3,2,1,0:T(8,128)(2,1)S(1)}, u32[]{:S(2)}, u32[]{:S(2)}) collective-permute-start(bf16[1,8,64,256]{3,2,1,0:T(8,128)(2,1)S(1)} %copy.99), channel_id=1, source_target_pairs={{0,8},{8,16},{16,24},{24,32},{32,40},{40,48},{48,56},{1,9},{9,17},... | collective-permute-start | bytes 786440 | tf_op jit(solution)/shard_map/ppermute | solution.py:15
  98.5 0.9 copy-done.1
  100.0 1.9 collective-permute-start.7
  101.9 4.8 %collective-permute-start.6 = (bf16[3,1,64,256]{3,2,1,0:T(8,128)(2,1)S(1)}, bf16[3,1,64,256]{3,2,1,0:T(8,128)(2,1)S(1)}, u32[]{:S(2)}, u32[]{:S(2)}) collective-permute-start(bf16[3,1,64,256]{3,2,1,0:T(8,128)(2,1)S(1)} %get-tuple-element.39), channel_id=1, source_target_pairs={{0,1},{1,2},{2,3},{3,4},{4,5},{5,6},{6,7},{8,9},{9,10},{10,11},{11... | collective-permute-start | bytes 294920 | tf_op jit(solution)/shard_map/ppermute | solution.py:15
  106.9 1.4 copy.97
  109.2 0.9 fusion.240
  116.3 180.5 %all-reduce.4.cloned.1.call-done = f32[27,32,256]{2,1,0:T(8,128)} async-done(((f32[27,32,256]{2,1,0:T(8,128)}), f32[27,32,256]{2,1,0:T(8,128)}) %all-reduce.4.cloned.1.call-update) | async-done | bytes 884752 | tf_op jit(solution)/shard_map/psum | solution.py:65
  296.8 2.2 broadcast_multiply_fusion
  299.0 1.5 convert_element_type.21
  (191 shorter events, 29.7 us)
Async XLA Ops:
  8.0 5.6 %collective-permute-start = (bf16[1,8,64,32]{2,3,1,0:T(8,128)(2,1)}, bf16[1,8,64,32]{2,3,1,0:T(8,128)(2,1)S(1)}, u32[]{:S(2)}, u32[]{:S(2)}) collective-permute-start(bf16[1,8,64,32]{2,3,1,0:T(8,128)(2,1)} %param.3), channel_id=1, source_target_pairs={{0,8},{8,16},{16,24},{24,32},{32,40},{40,48},{48,56},{1,9},{9,17},... | collective-permute-start | bytes 98312 | tf_op jit(solution)/shard_map/ppermute | solution.py:15
  11.7 5.8 %collective-permute-start.1 = (bf16[1,8,64,32]{2,3,1,0:T(8,128)(2,1)}, bf16[1,8,64,32]{2,3,1,0:T(8,128)(2,1)S(1)}, u32[]{:S(2)}, u32[]{:S(2)}) collective-permute-start(bf16[1,8,64,32]{2,3,1,0:T(8,128)(2,1)} %param.3), channel_id=1, source_target_pairs={{8,0},{16,8},{24,16},{32,24},{40,32},{48,40},{56,48},{9,1},{17,9},... | collective-permute-start | bytes 98312 | tf_op jit(solution)/shard_map/ppermute | solution.py:16
  17.5 21.3 %collective-permute-start.3 = (bf16[3,1,64,32]{2,3,1,0:T(8,128)(2,1)S(1)}, bf16[3,1,64,32]{2,3,1,0:T(8,128)(2,1)S(1)}, u32[]{:S(2)}, u32[]{:S(2)}) collective-permute-start(bf16[3,1,64,32]{2,3,1,0:T(8,128)(2,1)S(1)} %get-tuple-element.69), channel_id=1, source_target_pairs={{1,0},{2,1},{3,2},{4,3},{5,4},{6,5},{7,6},{9,8},{10,9},{11,10},{12... | collective-permute-start | bytes 36872 | tf_op jit(solution)/shard_map/ppermute | solution.py:16
  19.6 19.2 %collective-permute-start.2 = (bf16[3,1,64,32]{2,3,1,0:T(8,128)(2,1)S(1)}, bf16[3,1,64,32]{2,3,1,0:T(8,128)(2,1)S(1)}, u32[]{:S(2)}, u32[]{:S(2)}) collective-permute-start(bf16[3,1,64,32]{2,3,1,0:T(8,128)(2,1)S(1)} %get-tuple-element.68), channel_id=1, source_target_pairs={{0,1},{1,2},{2,3},{3,4},{4,5},{5,6},{6,7},{8,9},{9,10},{10,11},{11... | collective-permute-start | bytes 36872 | tf_op jit(solution)/shard_map/ppermute | solution.py:15
  24.9 11.5 %copy-start.2 = (bf16[1,8,64,32]{2,3,1,0:T(8,128)(2,1)S(1)}, bf16[1,8,64,32]{2,3,1,0:T(8,128)(2,1)}, u32[]{:S(2)}) copy-start(bf16[1,8,64,32]{2,3,1,0:T(8,128)(2,1)} %param.3) | copy-start | bytes 98308
  26.4 59.8 %all-to-all-start = ((bf16[8,2,8192]{2,1,0:T(2,128)(2,1)}), bf16[8,2,8192]{2,1,0:T(2,128)(2,1)S(1)}, u32[]{:S(2)}, u32[]{:S(2)}) async-start(bf16[8,2,8192]{2,1,0:T(2,128)(2,1)} %reshape.439), calls=%async_computation.1 | async-start | bytes 524288 | tf_op jit(solution)/shard_map/all_to_all | solution.py:41
  36.4 260.3 %all-reduce.4.cloned.1.call-start = ((), (), s32[]{:S(2)}) async-start(), calls=%async_computation.3 | async-start | bytes 1769472 | tf_op jit(solution)/shard_map/psum | solution.py:65
  38.8 0.6 copy-start.27
  39.4 0.6 copy-start.28
  40.1 1.4 copy-start
  43.3 10.3 %copy-start.6 = (bf16[1,8,64,32]{2,3,1,0:T(8,128)(2,1)S(1)}, bf16[1,8,64,32]{2,3,1,0:T(8,128)(2,1)}, u32[]{:S(2)}) copy-start(bf16[1,8,64,32]{2,3,1,0:T(8,128)(2,1)} %get-tuple-element.52) | copy-start | bytes 98308
  47.5 25.0 %copy-start.5 = (bf16[1,8,64,32]{2,3,1,0:T(8,128)(2,1)S(1)}, bf16[1,8,64,32]{2,3,1,0:T(8,128)(2,1)}, u32[]{:S(2)}) copy-start(bf16[1,8,64,32]{2,3,1,0:T(8,128)(2,1)} %get-tuple-element.47) | copy-start | bytes 98308
  48.9 25.8 %copy-start.4 = (bf16[1,8,64,32]{2,3,1,0:T(8,128)(2,1)S(1)}, bf16[1,8,64,32]{2,3,1,0:T(8,128)(2,1)}, u32[]{:S(2)}) copy-start(bf16[1,8,64,32]{2,3,1,0:T(8,128)(2,1)} %get-tuple-element.46) | copy-start | bytes 98308
  54.2 21.4 %copy-start.3 = (bf16[1,8,64,32]{2,3,1,0:T(8,128)(2,1)S(1)}, bf16[1,8,64,32]{2,3,1,0:T(8,128)(2,1)}, u32[]{:S(2)}) copy-start(bf16[1,8,64,32]{2,3,1,0:T(8,128)(2,1)} %get-tuple-element.45) | copy-start | bytes 98308
  75.5 2.9 copy-start.14
  78.1 0.8 copy-start.18
  78.3 0.8 copy-start.10
  78.8 0.8 copy-start.11
  79.1 0.8 copy-start.12
  79.6 0.8 copy-start.13
  79.9 0.8 copy-start.15
  80.3 0.8 copy-start.16
  80.6 0.8 copy-start.19
  81.1 0.8 copy-start.22
  81.4 0.8 copy-start.8
  81.9 0.8 copy-start.17
  82.1 0.8 copy-start.20
  82.6 0.8 copy-start.21
  82.9 0.8 copy-start.23
  83.4 0.8 copy-start.24
  84.2 0.8 copy-start.25
  84.4 0.8 copy-start.26
  84.9 0.8 copy-start.7
  86.9 13.0 %collective-permute-start.5 = (bf16[1,8,64,256]{3,2,1,0:T(8,128)(2,1)S(1)}, bf16[1,8,64,256]{3,2,1,0:T(8,128)(2,1)S(1)}, u32[]{:S(2)}, u32[]{:S(2)}) collective-permute-start(bf16[1,8,64,256]{3,2,1,0:T(8,128)(2,1)S(1)} %copy.99), channel_id=1, source_target_pairs={{8,0},{16,8},{24,16},{32,24},{40,32},{48,40},{56,48},{9,1},{17,9},... | collective-permute-start | bytes 786440 | tf_op jit(solution)/shard_map/ppermute | solution.py:16
  88.8 11.1 %collective-permute-start.4 = (bf16[1,8,64,256]{3,2,1,0:T(8,128)(2,1)S(1)}, bf16[1,8,64,256]{3,2,1,0:T(8,128)(2,1)S(1)}, u32[]{:S(2)}, u32[]{:S(2)}) collective-permute-start(bf16[1,8,64,256]{3,2,1,0:T(8,128)(2,1)S(1)} %copy.99), channel_id=1, source_target_pairs={{0,8},{8,16},{16,24},{24,32},{32,40},{40,48},{48,56},{1,9},{9,17},... | collective-permute-start | bytes 786440 | tf_op jit(solution)/shard_map/ppermute | solution.py:15
  97.6 1.9 copy-start.9
  98.5 0.9 copy-start.1
  99.4 199.5 %reduce-scatter.2.cloned.1.call-start = ((), (), s32[]{:S(2)}) async-start(), calls=%async_computation.2 | async-start | bytes 1179648 | tf_op jit(solution)/shard_map/reduce_scatter | solution.py:36
  100.0 8.3 %collective-permute-start.7 = (bf16[3,1,64,256]{3,2,1,0:T(8,128)(2,1)S(1)}, bf16[3,1,64,256]{3,2,1,0:T(8,128)(2,1)S(1)}, u32[]{:S(2)}, u32[]{:S(2)}) collective-permute-start(bf16[3,1,64,256]{3,2,1,0:T(8,128)(2,1)S(1)} %get-tuple-element.40), channel_id=1, source_target_pairs={{1,0},{2,1},{3,2},{4,3},{5,4},{6,5},{7,6},{9,8},{10,9},{11,10},{12... | collective-permute-start | bytes 294920 | tf_op jit(solution)/shard_map/ppermute | solution.py:16
  101.9 6.7 %collective-permute-start.6 = (bf16[3,1,64,256]{3,2,1,0:T(8,128)(2,1)S(1)}, bf16[3,1,64,256]{3,2,1,0:T(8,128)(2,1)S(1)}, u32[]{:S(2)}, u32[]{:S(2)}) collective-permute-start(bf16[3,1,64,256]{3,2,1,0:T(8,128)(2,1)S(1)} %get-tuple-element.39), channel_id=1, source_target_pairs={{0,1},{1,2},{2,3},{3,4},{4,5},{5,6},{6,7},{8,9},{9,10},{10,11},{11... | collective-permute-start | bytes 294920 | tf_op jit(solution)/shard_map/ppermute | solution.py:15
Sparse Core Ops, SparseCore 0:
  99.6 197.1 all-reduce.3
Sparse Core Ops, SparseCore 1:
  108.4 35.3 reduce-scatter.1
